TPU v7x, 32 devices: a whole 2x2x4 slice. The times are simulated.
32 devices in a mesh: seq: 16 (over z, x, core), tp: 2 (over y).
Axes of the slice: x: 2, y: 2, z: 4, core: 2. Of those that a mesh axis runs over, the one named last changes fastest.
Arguments:
- normed_input: bfloat16 [2048, 4096], P(('seq', 'tp')), may hold values from -6 to 6
- output_gradient: bfloat16 [2048, 14336], P('seq', 'tp'), may hold values from -0.75 to 0.75
- adapter_down: bfloat16 [64, 16, 4096], P('seq', None, 'tp'), may hold values from -0.09375 to 0.09375
- adapter_up: bfloat16 [64, 16, 14336], P('seq', None, 'tp'), may hold values from -1.5 to 1.5
- adapter_of_block: int32 [16], P('seq'), may hold values from 0 to 63
- live_per_block: int32 [16], P('seq'), may hold values from 32 to 128, as said below
- adapter_home_row: int32 [64], replicated, may hold values from 0 to 63, each once
Outputs:
- adapter_output: bfloat16 [2048, 14336], P('seq', 'tp')
- input_gradient: bfloat16 [2048, 4096], P(('seq', 'tp'))
- down_gradient: float32 [64, 16, 4096], P('seq', None, 'tp')
- up_gradient: float32 [64, 16, 14336], P('seq', None, 'tp')
Inputs may be any that keep to these rules, and one draw needn't show every extreme that they name: `live_per_block`: every eighth block, counting from block 0, is full. `adapter_home_row`: each row appears once.
All inputs are finite; a program needn't handle non-finite values.
Results may differ from a plain program's by a relative error of at most 0.0051.
Values may be sent and summed in bfloat16 or wider, within the bound.
A program may use at most 128 MiB of HBM per device.

v0:
```python
import jax
import jax.numpy as jnp
from jax import lax
from jax.sharding import PartitionSpec as P

adapter_scale = 2.0


def per_device(
    normed_input,
    output_gradient,
    adapter_down,
    adapter_up,
    adapter_of_block,
    live_per_block,
    adapter_home_row,
):
    seq_count = lax.axis_size("seq")
    total_blocks = adapter_of_block.shape[0]
    token_rows = output_gradient.shape[0]
    block_length = token_rows // total_blocks
    adapters = adapter_home_row.shape[0]
    rank_projected = adapter_down.shape[1]
    width_slice = adapter_down.shape[2]
    hidden_slice = adapter_up.shape[2]
    all_a, all_b = (
        lax.all_gather(adapter_down, "seq", axis=0, tiled=True),
        lax.all_gather(adapter_up, "seq", axis=0, tiled=True),
    )
    chosen = (adapter_of_block[:, None] == jnp.arange(adapters, dtype=jnp.int32)[None, :]).astype(
        jnp.float32
    )
    chosen_low = chosen.astype(jnp.bfloat16)
    pick_a = jnp.einsum(
        "ba,ard->brd", chosen_low, all_a, preferred_element_type=jnp.float32
    ).astype(jnp.bfloat16)
    pick_b = jnp.einsum(
        "ba,arf->brf", chosen_low, all_b, preferred_element_type=jnp.float32
    ).astype(jnp.bfloat16)
    token_live_mask = (
        jnp.arange(block_length, dtype=jnp.int32)[None, :] < live_per_block[:, None]
    ).astype(jnp.float32)[:, :, None]
    g_blocks = output_gradient.reshape(total_blocks, block_length, hidden_slice)
    back_part = jnp.einsum("btf,brf->btr", g_blocks, pick_b, preferred_element_type=jnp.float32)
    back_part = back_part.reshape(total_blocks, block_length * rank_projected)
    x_tensor = lax.all_to_all(normed_input, "tp", split_axis=1, concat_axis=0, tiled=True)
    x_blocks = x_tensor.reshape(total_blocks, block_length, width_slice)
    down_part = jnp.einsum("btd,brd->btr", x_blocks, pick_a, preferred_element_type=jnp.float32)
    down_part = down_part.reshape(total_blocks, block_length * rank_projected)
    down_sum, backward_total = lax.psum((down_part, back_part), "tp")
    down_reduced = (
        down_sum.reshape(total_blocks, block_length, rank_projected) * token_live_mask
    ).astype(jnp.bfloat16)
    backward_reduced = (
        adapter_scale
        * backward_total.reshape(total_blocks, block_length, rank_projected)
        * token_live_mask
    ).astype(jnp.bfloat16)
    grad_tensor = jnp.einsum(
        "btr,brd->btd", backward_reduced, pick_a, preferred_element_type=jnp.float32
    )
    grad_tensor = grad_tensor.astype(jnp.bfloat16).reshape(token_rows, width_slice)
    input_gradient = lax.all_to_all(grad_tensor, "tp", split_axis=0, concat_axis=1, tiled=True)
    grad_a_blocks = jnp.einsum(
        "btr,btd->brd", backward_reduced, x_blocks, preferred_element_type=jnp.float32
    )
    adapter_output = adapter_scale * jnp.einsum(
        "btr,brf->btf", down_reduced, pick_b, preferred_element_type=jnp.float32
    )
    adapter_output = adapter_output.astype(jnp.bfloat16).reshape(token_rows, hidden_slice)
    up_gradient_blocks = adapter_scale * jnp.einsum(
        "btr,btf->brf", down_reduced, g_blocks, preferred_element_type=jnp.float32
    )
    block_row = jnp.dot(
        chosen, adapter_home_row.astype(jnp.float32), precision=lax.Precision.HIGHEST
    )
    slots_each = adapters // seq_count
    my_rows = (lax.axis_index("seq") * slots_each + jnp.arange(slots_each, dtype=jnp.int32)).astype(
        jnp.float32
    )
    piece_a = lax.all_gather(grad_a_blocks, "seq", axis=0, tiled=True)
    piece_b = lax.all_gather(up_gradient_blocks, "seq", axis=0, tiled=True)
    piece_rows = lax.all_gather(block_row, "seq", axis=0, tiled=True)
    match = (piece_rows[:, None] == my_rows[None, :]).astype(jnp.float32)
    following_down = jnp.einsum("ns,nrd->srd", match, piece_a, precision=lax.Precision.HIGHEST)
    following_up = jnp.einsum("ns,nrf->srf", match, piece_b, precision=lax.Precision.HIGHEST)
    return (adapter_output, input_gradient, following_down, following_up)


def solution(mesh):
    placed = (
        P(("seq", "tp"), None),
        P("seq", "tp"),
        P("seq", None, "tp"),
        P("seq", None, "tp"),
        P("seq"),
        P("seq"),
        P(),
    )
    return jax.shard_map(
        per_device,
        mesh=mesh,
        in_specs=placed,
        out_specs=(
            P("seq", "tp"),
            P(("seq", "tp"), None),
            P("seq", None, "tp"),
            P("seq", None, "tp"),
        ),
        check_vma=False,
    )
```

profile of v0, /device:TPU:0, one launch (start us, length us, event | category | flops | bytes accessed | tf_op | source)
XLA Modules:
  0.0 334.9 jit_solution(5447570768813441117)
XLA Ops:
  7.2 0.7 all-gather.7.cloned.1.call-update
  8.0 0.7 all-gather.9.cloned.1.call-update
  8.7 1.9 copy.62
  10.5 4.3 %all-to-all-start = ((bf16[64,2,2048]{2,0,1:T(8,128)(2,1)}), bf16[64,2,2048]{2,0,1:T(8,128)(2,1)S(1)}, u32[]{:S(2)}, u32[]{:S(2)}) async-start(bf16[64,2,2048]{2,0,1:T(8,128)(2,1)} %bitcast.50), calls=%async_computation | async-start | bytes 1048576 | tf_op jit(solution)/shard_map/all_to_all | solution.py:46
  16.5 46.8 %all-gather.7.cloned.1.call-done = bf16[64,16,2048]{2,1,0:T(8,128)(2,1)} async-done(((bf16[4,16,2048]{2,1,0:T(8,128)(2,1)}), bf16[64,16,2048]{2,1,0:T(8,128)(2,1)}) %all-gather.7.cloned.1.call-update) | async-done | bytes 4194320 | tf_op jit(solution)/shard_map/all_gather | solution.py:27
  63.3 6.7 %fusion.5 = bf16[1,16,2048]{2,0,1:T(2,128)(2,1)S(1)} fusion(bf16[64,16,2048]{2,1,0:T(8,128)(2,1)} %all-gather.7.cloned.1.call-done, s32[]{:T(128)} %bitcast.51), kind=kOutput, calls=%fused_computation.7 | convolution fusion | flops 4194496 | bytes 4259844 | tf_op jit(solution)/shard_map/ba,ard->brd/dot_general | solution.py:34
  70.4 107.1 %all-gather.9.cloned.1.call-done = bf16[64,16,7168]{2,1,0:T(8,128)(2,1)} async-done(((bf16[4,16,7168]{2,1,0:T(8,128)(2,1)}), bf16[64,16,7168]{2,1,0:T(8,128)(2,1)}) %all-gather.9.cloned.1.call-update) | async-done | bytes 14680080 | tf_op jit(solution)/shard_map/all_gather | solution.py:28
  177.5 20.9 %fusion = bf16[1,16,7168]{2,0,1:T(2,128)(2,1)S(1)} fusion(bf16[64,16,7168]{2,1,0:T(8,128)(2,1)} %all-gather.9.cloned.1.call-done, s32[]{:T(128)} %bitcast.52), kind=kOutput, calls=%fused_computation | convolution fusion | flops 14680256 | bytes 14909444 | tf_op jit(solution)/shard_map/ba,arf->brf/dot_general | solution.py:37
  199.2 8.1 %all-reduce.1 = (f32[1,2048]{1,0:T(1,128)S(1)}, f32[1,2048]{1,0:T(1,128)S(1)}) all-reduce(f32[1,2048]{1,0:T(1,128)S(1)} %reshape.142, f32[1,2048]{1,0:T(1,128)S(1)} %reshape.143), channel_id=1, replica_groups=mesh['seq'=16,'tp'=2] {'tp'}, use_global_device_ids=true, to_apply=%region_0.0 | all-reduce | flops 4096 | bytes 32768 | tf_op jit(solution)/shard_map/psum | solution.py:50
  207.4 0.9 fusion.24
  208.4 1.2 convolution_multiply_fusion.1
  210.2 0.6 fusion.19
  210.8 1.4 dynamic-update-slice
  212.2 30.0 %all-reduce = f32[16]{0:T(128)S(1)} all-reduce(f32[16]{0:T(128)S(1)} %dynamic-update-slice), channel_id=1, replica_groups=mesh['seq'=16,'tp'=2] {'seq'}, use_global_device_ids=true, to_apply=%add | all-reduce | flops 16 | bytes 128
  242.2 1.1 convolution_convert_fusion
  243.3 3.7 %all-to-all-start.1 = ((bf16[2,64,2048]{2,1,0:T(8,128)(2,1)}), bf16[2,64,2048]{2,1,0:T(8,128)(2,1)S(1)}, u32[]{:S(2)}, u32[]{:S(2)}) async-start(bf16[2,64,2048]{2,1,0:T(8,128)(2,1)} %bitcast.10), calls=%async_computation.1 | async-start | bytes 1048576 | tf_op jit(solution)/shard_map/all_to_all | solution.py:63
  247.0 1.8 fusion.2
  248.9 6.0 %all-to-all-done.1 = bf16[2,64,2048]{2,1,0:T(8,128)(2,1)S(1)} async-done(((bf16[2,64,2048]{2,1,0:T(8,128)(2,1)}), bf16[2,64,2048]{2,1,0:T(8,128)(2,1)S(1)}, u32[]{:S(2)}, u32[]{:S(2)}) %all-to-all-start.1) | async-done | bytes 524320 | tf_op jit(solution)/shard_map/all_to_all | solution.py:63
  254.9 0.8 copy.46
  255.7 3.6 %fusion.7 = f32[4,16,2048]{2,0,1:T(4,128)S(1)} fusion(f32[16,16,2048]{2,1,0:T(8,128)} %bitcast.59, f32[16]{0:T(128)S(1)} %all-reduce, f32[4]{0:T(128)S(1)} %add_convert_fusion), kind=kOutput, calls=%fused_computation.10 | convolution fusion | flops 25165888 | bytes 2621520 | tf_op jit(solution)/shard_map/ns,nrd->srd/dot_general | solution.py:85
  259.3 1.1 copy.37
  260.4 56.1 %all-gather.13.cloned.1.call-done = f32[256,7168]{1,0:T(8,128)} async-done(((f32[16,7168]{1,0:T(8,128)}), f32[256,7168]{1,0:T(8,128)}) %all-gather.13.cloned.1.call-update) | async-done | bytes 7340048 | tf_op jit(solution)/shard_map/all_gather | solution.py:82
  316.5 9.5 %fusion.3 = f32[4,16,7168]{2,0,1:T(4,128)S(1)} fusion(f32[16,16,7168]{2,1,0:T(8,128)} %bitcast.56, f32[16]{0:T(128)S(1)} %all-reduce, f32[4]{0:T(128)S(1)} %add_convert_fusion), kind=kOutput, calls=%fused_computation.5 | convolution fusion | flops 88080448 | bytes 9175120 | tf_op jit(solution)/shard_map/ns,nrf->srf/dot_general | solution.py:86
  326.1 2.3 copy.38
  (32 shorter events, 2.6 us)
Async XLA Ops:
  7.2 191.2 %copy-start = (bf16[128,7168]{1,0:T(8,128)(2,1)S(1)}, bf16[128,7168]{1,0:T(8,128)(2,1)}, u32[]{:S(2)}) copy-start(bf16[128,7168]{1,0:T(8,128)(2,1)} %param.8) | copy-start | bytes 5505028
  7.2 56.1 %all-gather.7.cloned.1.call-start = ((), (), s32[]{:S(2)}) async-start(), calls=%async_computation.2 | async-start | bytes 4456448 | tf_op jit(solution)/shard_map/all_gather | solution.py:27
  7.9 169.6 %all-gather.9.cloned.1.call-start = ((), (), s32[]{:S(2)}) async-start(), calls=%async_computation.3 | async-start | bytes 15597568 | tf_op jit(solution)/shard_map/all_gather | solution.py:28
  10.5 59.4 %all-to-all-start = ((bf16[64,2,2048]{2,0,1:T(8,128)(2,1)}), bf16[64,2,2048]{2,0,1:T(8,128)(2,1)S(1)}, u32[]{:S(2)}, u32[]{:S(2)}) async-start(bf16[64,2,2048]{2,0,1:T(8,128)(2,1)} %bitcast.50), calls=%async_computation | async-start | bytes 1048576 | tf_op jit(solution)/shard_map/all_to_all | solution.py:46
  14.8 240.9 %all-gather.11.cloned.1.call-start = ((), (), s32[]{:S(2)}) async-start(), calls=%async_computation.4 | async-start | bytes 2228224 | tf_op jit(solution)/shard_map/all_gather | solution.py:81
  198.4 11.3 %copy-start.2 = (u32[32]{0:T(128)S(1)}, u32[32]{0:T(128)}, u32[]{:S(2)}) copy-start(u32[32]{0:T(128)} %constant.20) | copy-start | bytes 388
  198.4 11.9 %copy-start.1 = (s32[64]{0:T(128)S(1)}, s32[64]{0:T(128)}, u32[]{:S(2)}) copy-start(s32[64]{0:T(128)} %param.13) | copy-start | bytes 772
  208.3 108.2 %all-gather.13.cloned.1.call-start = ((), (), s32[]{:S(2)}) async-start(), calls=%async_computation.5 | async-start | bytes 7798784 | tf_op jit(solution)/shard_map/all_gather | solution.py:82
  243.3 11.6 %all-to-all-start.1 = ((bf16[2,64,2048]{2,1,0:T(8,128)(2,1)}), bf16[2,64,2048]{2,1,0:T(8,128)(2,1)S(1)}, u32[]{:S(2)}, u32[]{:S(2)}) async-start(bf16[2,64,2048]{2,1,0:T(8,128)(2,1)} %bitcast.10), calls=%async_computation.1 | async-start | bytes 1048576 | tf_op jit(solution)/shard_map/all_to_all | solution.py:63
Sparse Core Ops, SparseCore 0:
  10.1 53.0 all-gather.6
  65.6 111.8 all-gather.8
  208.4 38.7 all-gather.10
  249.9 66.5 all-gather.12
where the time goes:
time: 335 us
  waiting for transfers between devices  217 us (65%)
  matrix products  46.5 us (14%)
  blocking collectives  38 us (11%)
  between operations  15.2 us (5%)
  local copies, waits for them, and re-layouts  9.04 us (3%)
  starting transfers between devices  8.09 us (2%)
    all_gather x1, waiting for transfers between devices, per_device(): lax.all_gather(adapter_up, 'seq', axis=0, tiled=True)  107 us
    all_gather x1, waiting for transfers between devices, per_device(): piece_b = lax.all_gather(up_gradient_blocks, 'seq', axis=0, tiled=True)  56.1 us
    all_gather x1, waiting for transfers between devices, per_device(): lax.all_gather(adapter_down, 'seq', axis=0, tiled=True)  46.8 us
    unnamed x1, blocking collectives  30 us
    dot_general x1, matrix products, per_device(): jnp.einsum('ba,arf->brf', chosen_low, all_b, preferred_element_type=jnp.f...  20.9 us
    dot_general x1, matrix products, per_device(): jnp.einsum('ns,nrf->srf', match, piece_b, precision=lax.Precision.HIGHEST)  9.53 us
    psum x1, blocking collectives, per_device(): down_sum, backward_total = lax.psum((down_part, back_part), 'tp')  8.06 us
    dot_general x1, matrix products, per_device(): jnp.einsum('ba,ard->brd', chosen_low, all_a, preferred_element_type=jnp.f...  6.7 us
  transfers between devices with their start and end apart: 6, of which 4 were waited for; matrix products, arithmetic and copies ran while one was open for 6% of the time, Pallas kernels for 0%

commit v1 on v0

--- a/solution.py
+++ b/solution.py
@@ -2,8 +2,35 @@
 import jax.numpy as jnp
 from jax import lax
 from jax.sharding import PartitionSpec as P
+from jax.lax import axis_index, axis_size, ppermute
 
 adapter_scale = 2.0
+
+
+def follow_sums_all(piece_in, m):
+    extra, fresh, piece_out = (axis_size("seq"), axis_index("seq"), piece_in.shape[0])
+    tray = []
+    s = 0
+    while s < extra:
+        tray.append((s, (s + 1) % extra))
+        s = s + 1
+    leaves = []
+    s = 0
+    while s < extra:
+        leaves.append((s, (s - 1) % extra))
+        s += 1
+    current_value = extra // 2
+    z = z1 = piece_in
+    v_now = m(piece_in, fresh * piece_out)
+    i = 1
+    while i < current_value + 1:
+        z = ppermute(z, "seq", tray)
+        if i < extra - current_value:
+            z1 = ppermute(z1, "seq", leaves)
+            v_now = v_now + m(z1, (fresh + i) % extra * piece_out)
+        v_now = v_now + m(z, (fresh - i) % extra * piece_out)
+        i += 1
+    return v_now
 
 
 def per_device(
@@ -79,11 +106,18 @@
         jnp.float32
     )
     piece_a = lax.all_gather(grad_a_blocks, "seq", axis=0, tiled=True)
-    piece_b = lax.all_gather(up_gradient_blocks, "seq", axis=0, tiled=True)
     piece_rows = lax.all_gather(block_row, "seq", axis=0, tiled=True)
     match = (piece_rows[:, None] == my_rows[None, :]).astype(jnp.float32)
     following_down = jnp.einsum("ns,nrd->srd", match, piece_a, precision=lax.Precision.HIGHEST)
-    following_up = jnp.einsum("ns,nrf->srf", match, piece_b, precision=lax.Precision.HIGHEST)
+    following_up = follow_sums_all(
+        up_gradient_blocks,
+        lambda own_block, offset: jnp.einsum(
+            "ns,nrf->srf",
+            lax.dynamic_slice_in_dim(match, offset, own_block.shape[0], axis=0),
+            own_block,
+            precision=lax.Precision.HIGHEST,
+        ),
+    )
     return (adapter_output, input_gradient, following_down, following_up)
 
 

time: 335 us -> 351 us (1.048)
  starting transfers between devices: 8.09 us -> 46.3 us
  waiting for transfers between devices: 217 us -> 196 us
  matrix products: 46.5 us -> 36.1 us
  other arithmetic: 0.67 us -> 7.12 us
  blocking collectives: 38 us -> 42.9 us
    all_gather x1 -> x0, waiting for transfers between devices: 56.1 us -> none  [per_device(): piece_b = lax.all_gather(up_gradient_blocks, 'seq', axis=0, tiled=True)]
    ppermute x0 -> x15, starting transfers between devices: none -> 36.5 us  [the longest x8 21.4 us: follow_sums_all(): z = ppermute(z, 'seq', tray)]
    ppermute x0 -> x15, waiting for transfers between devices: none -> 33.3 us  [the longest x8 33.2 us: follow_sums_all(): z = ppermute(z, 'seq', tray)]
    dot_general x1 -> x0, matrix products: 9.53 us -> none  [per_device(): jnp.einsum('ns,nrf->srf', match, piece_b, precision=lax.Precision.HIGHEST)]
    add x0 -> x1, other arithmetic: none -> 6.34 us  [follow_sums_all(): v_now = v_now + m(z, (fresh - i) % extra * piece_out)]
    unnamed x1, blocking collectives: 30 us -> 34.9 us
  transfers between devices with their start and end apart: 6 -> 20, of which waited for: 4 -> 9; matrix products, arithmetic and copies ran while one was open for 6% -> 7% of each run, Pallas kernels for 0% -> 0%
where the time goes in v1:
time: 351 us
  waiting for transfers between devices  196 us (56%)
  starting transfers between devices  46.3 us (13%)
  blocking collectives  42.9 us (12%)
  matrix products  36.1 us (10%)
  between operations  15.4 us (4%)
  local copies, waits for them, and re-layouts  7.21 us (2%)
  other arithmetic  7.12 us (2%)
    all_gather x1, waiting for transfers between devices, per_device(): lax.all_gather(adapter_up, 'seq', axis=0, tiled=True)  107 us
    all_gather x1, waiting for transfers between devices, per_device(): lax.all_gather(adapter_down, 'seq', axis=0, tiled=True)  46.8 us
    unnamed x1, blocking collectives  34.9 us
    ppermute x8, waiting for transfers between devices, follow_sums_all(): z = ppermute(z, 'seq', tray)  33.2 us
    ppermute x8, starting transfers between devices, follow_sums_all(): z = ppermute(z, 'seq', tray)  21.4 us
    dot_general x1, matrix products, per_device(): jnp.einsum('ba,arf->brf', chosen_low, all_b, preferred_element_type=jnp.f...  20.9 us
    ppermute x7, starting transfers between devices, follow_sums_all(): z1 = ppermute(z1, 'seq', leaves)  15.1 us
    psum x1, blocking collectives, per_device(): down_sum, backward_total = lax.psum((down_part, back_part), 'tp')  8.06 us
  transfers between devices with their start and end apart: 20, of which 9 were waited for; matrix products, arithmetic and copies ran while one was open for 7% of the time, Pallas kernels for 0%

profile of v1, /device:TPU:0, one launch (start us, length us, event | category | flops | bytes accessed | tf_op | source)
XLA Modules:
  0.0 350.7 jit_solution(7498619708754323797)
XLA Ops:
  10.5 4.3 %all-to-all-start = ((bf16[64,2,2048]{2,0,1:T(8,128)(2,1)}), bf16[64,2,2048]{2,0,1:T(8,128)(2,1)S(1)}, u32[]{:S(2)}, u32[]{:S(2)}) async-start(bf16[64,2,2048]{2,0,1:T(8,128)(2,1)} %bitcast.95), calls=%async_computation | async-start | bytes 1048576 | tf_op jit(solution)/shard_map/all_to_all | solution.py:73
  16.5 46.8 %all-gather.5.cloned.1.call-done = bf16[64,16,2048]{2,1,0:T(8,128)(2,1)} async-done(((bf16[4,16,2048]{2,1,0:T(8,128)(2,1)}), bf16[64,16,2048]{2,1,0:T(8,128)(2,1)}) %all-gather.5.cloned.1.call-update) | async-done | bytes 4194320 | tf_op jit(solution)/shard_map/all_gather | solution.py:54
  63.3 6.7 %fusion.3 = bf16[1,16,2048]{2,0,1:T(2,128)(2,1)S(1)} fusion(bf16[64,16,2048]{2,1,0:T(8,128)(2,1)} %all-gather.5.cloned.1.call-done, s32[]{:T(128)} %bitcast.96), kind=kOutput, calls=%fused_computation.5 | convolution fusion | flops 4194496 | bytes 4259844 | tf_op jit(solution)/shard_map/ba,ard->brd/dot_general | solution.py:61
  70.4 107.1 %all-gather.7.cloned.1.call-done = bf16[64,16,7168]{2,1,0:T(8,128)(2,1)} async-done(((bf16[4,16,7168]{2,1,0:T(8,128)(2,1)}), bf16[64,16,7168]{2,1,0:T(8,128)(2,1)}) %all-gather.7.cloned.1.call-update) | async-done | bytes 14680080 | tf_op jit(solution)/shard_map/all_gather | solution.py:55
  177.5 20.9 %fusion = bf16[1,16,7168]{2,0,1:T(2,128)(2,1)S(1)} fusion(bf16[64,16,7168]{2,1,0:T(8,128)(2,1)} %all-gather.7.cloned.1.call-done, s32[]{:T(128)} %bitcast.97), kind=kOutput, calls=%fused_computation | convolution fusion | flops 14680256 | bytes 14909444 | tf_op jit(solution)/shard_map/ba,arf->brf/dot_general | solution.py:64
  199.2 8.1 %all-reduce.1 = (f32[1,2048]{1,0:T(1,128)S(1)}, f32[1,2048]{1,0:T(1,128)S(1)}) all-reduce(f32[1,2048]{1,0:T(1,128)S(1)} %reshape.269, f32[1,2048]{1,0:T(1,128)S(1)} %reshape.270), channel_id=1, replica_groups=mesh['seq'=16,'tp'=2] {'tp'}, use_global_device_ids=true, to_apply=%region_0.0 | all-reduce | flops 4096 | bytes 32768 | tf_op jit(solution)/shard_map/psum | solution.py:77
  207.8 4.4 %collective-permute-start = (f32[1,16,7168]{2,1,0:T(8,128)S(1)}, f32[1,16,7168]{2,1,0:T(8,128)}, u32[]{:S(2)}, u32[]{:S(2)}) collective-permute-start(f32[1,16,7168]{2,1,0:T(8,128)S(1)} %bitcast.106), channel_id=1, source_target_pairs={{0,30},{2,0},{4,2},{6,4},{8,6},{10,8},{12,10},{14,12},{16,14},{18,... | collective-permute-start | bytes 1376264 | tf_op jit(solution)/shard_map/ppermute | solution.py:29
  212.3 6.3 %collective-permute-done.1 = f32[1,16,7168]{2,1,0:T(8,128)S(1)} collective-permute-done((f32[1,16,7168]{2,1,0:T(8,128)S(1)}, f32[1,16,7168]{2,1,0:T(8,128)S(1)}, u32[]{:S(2)}, u32[]{:S(2)}) %collective-permute-start.1) | collective-permute-done | bytes 458784 | tf_op jit(solution)/shard_map/ppermute | solution.py:27
  219.3 3.8 %collective-permute-start.2 = (f32[1,16,7168]{2,1,0:T(8,128)}, f32[1,16,7168]{2,1,0:T(8,128)}, u32[]{:S(2)}, u32[]{:S(2)}) collective-permute-start(f32[1,16,7168]{2,1,0:T(8,128)} %collective-permute-done), channel_id=1, source_target_pairs={{0,30},{2,0},{4,2},{6,4},{8,6},{10,8},{12,10},{14,12},{16,14},{18,... | collective-permute-start | bytes 1376264 | tf_op jit(solution)/shard_map/ppermute | solution.py:29
  223.1 6.3 %collective-permute-done.3 = f32[1,16,7168]{2,1,0:T(8,128)} collective-permute-done((f32[1,16,7168]{2,1,0:T(8,128)S(1)}, f32[1,16,7168]{2,1,0:T(8,128)}, u32[]{:S(2)}, u32[]{:S(2)}) %collective-permute-start.3) | collective-permute-done | bytes 458784 | tf_op jit(solution)/shard_map/ppermute | solution.py:27
  230.4 3.7 %collective-permute-start.4 = (f32[1,16,7168]{2,1,0:T(8,128)}, f32[1,16,7168]{2,1,0:T(8,128)}, u32[]{:S(2)}, u32[]{:S(2)}) collective-permute-start(f32[1,16,7168]{2,1,0:T(8,128)} %collective-permute-done.2), channel_id=1, source_target_pairs={{0,30},{2,0},{4,2},{6,4},{8,6},{10,8},{12,10},{14,12},{16,14},{18,... | collective-permute-start | bytes 1376264 | tf_op jit(solution)/shard_map/ppermute | solution.py:29
  234.1 6.3 %collective-permute-done.5 = f32[1,16,7168]{2,1,0:T(8,128)} collective-permute-done((f32[1,16,7168]{2,1,0:T(8,128)}, f32[1,16,7168]{2,1,0:T(8,128)}, u32[]{:S(2)}, u32[]{:S(2)}) %collective-permute-start.5) | collective-permute-done | bytes 458784 | tf_op jit(solution)/shard_map/ppermute | solution.py:27
  240.3 2.3 collective-permute-start.7
  245.7 5.6 %collective-permute-done.7 = f32[1,16,7168]{2,1,0:T(8,128)} collective-permute-done((f32[1,16,7168]{2,1,0:T(8,128)}, f32[1,16,7168]{2,1,0:T(8,128)}, u32[]{:S(2)}, u32[]{:S(2)}) %collective-permute-start.7) | collective-permute-done | bytes 458784 | tf_op jit(solution)/shard_map/ppermute | solution.py:27
  251.4 4.5 %collective-permute-start.9 = (f32[1,16,7168]{2,1,0:T(8,128)}, f32[1,16,7168]{2,1,0:T(8,128)}, u32[]{:S(2)}, u32[]{:S(2)}) collective-permute-start(f32[1,16,7168]{2,1,0:T(8,128)} %collective-permute-done.7), channel_id=1, source_target_pairs={{0,2},{2,4},{4,6},{6,8},{8,10},{10,12},{12,14},{14,16},{16,18},{18... | collective-permute-start | bytes 1376264 | tf_op jit(solution)/shard_map/ppermute | solution.py:27
  256.5 5.9 %collective-permute-done.9 = f32[1,16,7168]{2,1,0:T(8,128)} collective-permute-done((f32[1,16,7168]{2,1,0:T(8,128)}, f32[1,16,7168]{2,1,0:T(8,128)}, u32[]{:S(2)}, u32[]{:S(2)}) %collective-permute-start.9) | collective-permute-done | bytes 458784 | tf_op jit(solution)/shard_map/ppermute | solution.py:27
  262.4 6.7 %collective-permute-start.11 = (f32[1,16,7168]{2,1,0:T(8,128)}, f32[1,16,7168]{2,1,0:T(8,128)}, u32[]{:S(2)}, u32[]{:S(2)}) collective-permute-start(f32[1,16,7168]{2,1,0:T(8,128)} %collective-permute-done.9), channel_id=1, source_target_pairs={{0,2},{2,4},{4,6},{6,8},{8,10},{10,12},{12,14},{14,16},{16,18},{18... | collective-permute-start | bytes 1376264 | tf_op jit(solution)/shard_map/ppermute | solution.py:27
  272.0 3.0 collective-permute-done.11
  274.9 6.1 %collective-permute-start.13 = (f32[1,16,7168]{2,1,0:T(8,128)}, f32[1,16,7168]{2,1,0:T(8,128)}, u32[]{:S(2)}, u32[]{:S(2)}) collective-permute-start(f32[1,16,7168]{2,1,0:T(8,128)} %collective-permute-done.11), channel_id=1, source_target_pairs={{0,2},{2,4},{4,6},{6,8},{8,10},{10,12},{12,14},{14,16},{16,18},{18... | collective-permute-start | bytes 1376264 | tf_op jit(solution)/shard_map/ppermute | solution.py:27
  281.1 34.9 %all-reduce = f32[16]{0:T(128)S(1)} all-reduce(f32[16]{0:T(128)S(1)} %dynamic-update-slice), channel_id=1, replica_groups=mesh['seq'=16,'tp'=2] {'seq'}, use_global_device_ids=true, to_apply=%add | all-reduce | flops 16 | bytes 128
  317.9 5.5 %all-to-all-start.1 = ((bf16[2,64,2048]{2,1,0:T(8,128)(2,1)}), bf16[2,64,2048]{2,1,0:T(8,128)(2,1)S(1)}, u32[]{:S(2)}, u32[]{:S(2)}) async-start(bf16[2,64,2048]{2,1,0:T(8,128)(2,1)} %bitcast.10), calls=%async_computation.1 | async-start | bytes 1048576 | tf_op jit(solution)/shard_map/all_to_all | solution.py:90
  325.3 7.0 %all-to-all-done.1 = bf16[2,64,2048]{2,1,0:T(8,128)(2,1)S(1)} async-done(((bf16[2,64,2048]{2,1,0:T(8,128)(2,1)}), bf16[2,64,2048]{2,1,0:T(8,128)(2,1)S(1)}, u32[]{:S(2)}, u32[]{:S(2)}) %all-to-all-start.1) | async-done | bytes 524320 | tf_op jit(solution)/shard_map/all_to_all | solution.py:90
  333.2 6.3 %multiply_add_fusion = f32[4,16,7168]{2,1,0:T(8,128)} fusion(f32[16,7168]{1,0:T(8,128)} %bitcast.48, f32[4]{0:T(128)S(1)} %get-tuple-element.37, f32[16,7168]{1,0:T(8,128)} %bitcast.46, f32[4]{0:T(128)S(1)} %get-tuple-element.23, f32[16,7168]{1,0:T(8,128)} %bitcast.44, f32[4]{0:T(128)S(1)} %get-tuple-element.24, f32[16,7168]{1,0:T(8,128)} %bitcast.42, ...), kind=kLoop, calls=%fused_computation.10 | loop fusion | flops 14221312 | bytes 9175296 | tf_op jit(solution)/shard_map/add | solution.py:31
  339.5 3.5 %fusion.5 = f32[4,16,2048]{2,0,1:T(4,128)S(1)} fusion(f32[16,16,2048]{2,1,0:T(8,128)} %bitcast.103, f32[4]{0:T(128)S(1)} %add_convert_fusion, f32[16]{0:T(128)S(1)} %all-reduce), kind=kOutput, calls=%fused_computation.8 | convolution fusion | flops 25165888 | bytes 2621520 | tf_op jit(solution)/shard_map/ns,nrd->srd/dot_general | solution.py:111
  (64 shorter events, 19.4 us)
Async XLA Ops:
  7.2 191.2 %copy-start = (bf16[128,7168]{1,0:T(8,128)(2,1)S(1)}, bf16[128,7168]{1,0:T(8,128)(2,1)}, u32[]{:S(2)}) copy-start(bf16[128,7168]{1,0:T(8,128)(2,1)} %param.8) | copy-start | bytes 5505028
  7.2 56.1 %all-gather.5.cloned.1.call-start = ((), (), s32[]{:S(2)}) async-start(), calls=%async_computation.2 | async-start | bytes 4456448 | tf_op jit(solution)/shard_map/all_gather | solution.py:54
  7.9 169.6 %all-gather.7.cloned.1.call-start = ((), (), s32[]{:S(2)}) async-start(), calls=%async_computation.3 | async-start | bytes 15597568 | tf_op jit(solution)/shard_map/all_gather | solution.py:55
  10.5 59.4 %all-to-all-start = ((bf16[64,2,2048]{2,0,1:T(8,128)(2,1)}), bf16[64,2,2048]{2,0,1:T(8,128)(2,1)S(1)}, u32[]{:S(2)}, u32[]{:S(2)}) async-start(bf16[64,2,2048]{2,0,1:T(8,128)(2,1)} %bitcast.95), calls=%async_computation | async-start | bytes 1048576 | tf_op jit(solution)/shard_map/all_to_all | solution.py:73
  14.8 324.7 %all-gather.9.cloned.1.call-start = ((), (), s32[]{:S(2)}) async-start(), calls=%async_computation.4 | async-start | bytes 2228224 | tf_op jit(solution)/shard_map/all_gather | solution.py:108
  199.0 70.2 %copy-start.4 = (u32[32]{0:T(128)S(1)}, u32[32]{0:T(128)}, u32[]{:S(2)}) copy-start(u32[32]{0:T(128)} %constant.119) | copy-start | bytes 388
  199.0 70.7 %copy-start.3 = (s32[64]{0:T(128)S(1)}, s32[64]{0:T(128)}, u32[]{:S(2)}) copy-start(s32[64]{0:T(128)} %param.13) | copy-start | bytes 772
  207.8 10.7 %collective-permute-start.1 = (f32[1,16,7168]{2,1,0:T(8,128)S(1)}, f32[1,16,7168]{2,1,0:T(8,128)S(1)}, u32[]{:S(2)}, u32[]{:S(2)}) collective-permute-start(f32[1,16,7168]{2,1,0:T(8,128)S(1)} %bitcast.105), channel_id=1, source_target_pairs={{0,2},{2,4},{4,6},{6,8},{8,10},{10,12},{12,14},{14,16},{16,18},{18... | collective-permute-start | bytes 1376264 | tf_op jit(solution)/shard_map/ppermute | solution.py:27
  207.8 11.0 %collective-permute-start = (f32[1,16,7168]{2,1,0:T(8,128)S(1)}, f32[1,16,7168]{2,1,0:T(8,128)}, u32[]{:S(2)}, u32[]{:S(2)}) collective-permute-start(f32[1,16,7168]{2,1,0:T(8,128)S(1)} %bitcast.106), channel_id=1, source_target_pairs={{0,30},{2,0},{4,2},{6,4},{8,6},{10,8},{12,10},{14,12},{16,14},{18,... | collective-permute-start | bytes 1376264 | tf_op jit(solution)/shard_map/ppermute | solution.py:29
  218.5 10.8 %collective-permute-start.3 = (f32[1,16,7168]{2,1,0:T(8,128)S(1)}, f32[1,16,7168]{2,1,0:T(8,128)}, u32[]{:S(2)}, u32[]{:S(2)}) collective-permute-start(f32[1,16,7168]{2,1,0:T(8,128)S(1)} %collective-permute-done.1), channel_id=1, source_target_pairs={{0,2},{2,4},{4,6},{6,8},{8,10},{10,12},{12,14},{14,16},{16,18},{18... | collective-permute-start | bytes 1376264 | tf_op jit(solution)/shard_map/ppermute | solution.py:27
  219.3 11.0 %collective-permute-start.2 = (f32[1,16,7168]{2,1,0:T(8,128)}, f32[1,16,7168]{2,1,0:T(8,128)}, u32[]{:S(2)}, u32[]{:S(2)}) collective-permute-start(f32[1,16,7168]{2,1,0:T(8,128)} %collective-permute-done), channel_id=1, source_target_pairs={{0,30},{2,0},{4,2},{6,4},{8,6},{10,8},{12,10},{14,12},{16,14},{18,... | collective-permute-start | bytes 1376264 | tf_op jit(solution)/shard_map/ppermute | solution.py:29
  229.3 11.0 %collective-permute-start.5 = (f32[1,16,7168]{2,1,0:T(8,128)}, f32[1,16,7168]{2,1,0:T(8,128)}, u32[]{:S(2)}, u32[]{:S(2)}) collective-permute-start(f32[1,16,7168]{2,1,0:T(8,128)} %collective-permute-done.3), channel_id=1, source_target_pairs={{0,2},{2,4},{4,6},{6,8},{8,10},{10,12},{12,14},{14,16},{16,18},{18... | collective-permute-start | bytes 1376264 | tf_op jit(solution)/shard_map/ppermute | solution.py:27
  230.4 13.2 %collective-permute-start.4 = (f32[1,16,7168]{2,1,0:T(8,128)}, f32[1,16,7168]{2,1,0:T(8,128)}, u32[]{:S(2)}, u32[]{:S(2)}) collective-permute-start(f32[1,16,7168]{2,1,0:T(8,128)} %collective-permute-done.2), channel_id=1, source_target_pairs={{0,30},{2,0},{4,2},{6,4},{8,6},{10,8},{12,10},{14,12},{16,14},{18,... | collective-permute-start | bytes 1376264 | tf_op jit(solution)/shard_map/ppermute | solution.py:29
  240.3 11.0 %collective-permute-start.7 = (f32[1,16,7168]{2,1,0:T(8,128)}, f32[1,16,7168]{2,1,0:T(8,128)}, u32[]{:S(2)}, u32[]{:S(2)}) collective-permute-start(f32[1,16,7168]{2,1,0:T(8,128)} %collective-permute-done.5), channel_id=1, source_target_pairs={{0,2},{2,4},{4,6},{6,8},{8,10},{10,12},{12,14},{14,16},{16,18},{18... | collective-permute-start | bytes 1376264 | tf_op jit(solution)/shard_map/ppermute | solution.py:27
  243.6 12.2 %collective-permute-start.6 = (f32[1,16,7168]{2,1,0:T(8,128)}, f32[1,16,7168]{2,1,0:T(8,128)S(1)}, u32[]{:S(2)}, u32[]{:S(2)}) collective-permute-start(f32[1,16,7168]{2,1,0:T(8,128)} %collective-permute-done.4), channel_id=1, source_target_pairs={{0,30},{2,0},{4,2},{6,4},{8,6},{10,8},{12,10},{14,12},{16,14},{18,... | collective-permute-start | bytes 1376264 | tf_op jit(solution)/shard_map/ppermute | solution.py:29
  251.4 11.1 %collective-permute-start.9 = (f32[1,16,7168]{2,1,0:T(8,128)}, f32[1,16,7168]{2,1,0:T(8,128)}, u32[]{:S(2)}, u32[]{:S(2)}) collective-permute-start(f32[1,16,7168]{2,1,0:T(8,128)} %collective-permute-done.7), channel_id=1, source_target_pairs={{0,2},{2,4},{4,6},{6,8},{8,10},{10,12},{12,14},{14,16},{16,18},{18... | collective-permute-start | bytes 1376264 | tf_op jit(solution)/shard_map/ppermute | solution.py:27
  255.8 62.1 %copy-start.2 = (f32[1,16,7168]{2,1,0:T(8,128)}, f32[1,16,7168]{2,1,0:T(8,128)S(1)}, u32[]{:S(2)}) copy-start(f32[1,16,7168]{2,1,0:T(8,128)S(1)} %collective-permute-done.6) | copy-start | bytes 1376260
  255.8 15.9 %collective-permute-start.8 = (f32[1,16,7168]{2,1,0:T(8,128)S(1)}, f32[1,16,7168]{2,1,0:T(8,128)}, u32[]{:S(2)}, u32[]{:S(2)}) collective-permute-start(f32[1,16,7168]{2,1,0:T(8,128)S(1)} %collective-permute-done.6), channel_id=1, source_target_pairs={{0,30},{2,0},{4,2},{6,4},{8,6},{10,8},{12,10},{14,12},{16,14},{18,... | collective-permute-start | bytes 1376264 | tf_op jit(solution)/shard_map/ppermute | solution.py:29
  262.4 12.5 %collective-permute-start.11 = (f32[1,16,7168]{2,1,0:T(8,128)}, f32[1,16,7168]{2,1,0:T(8,128)}, u32[]{:S(2)}, u32[]{:S(2)}) collective-permute-start(f32[1,16,7168]{2,1,0:T(8,128)} %collective-permute-done.9), channel_id=1, source_target_pairs={{0,2},{2,4},{4,6},{6,8},{8,10},{10,12},{12,14},{14,16},{16,18},{18... | collective-permute-start | bytes 1376264 | tf_op jit(solution)/shard_map/ppermute | solution.py:27
  271.7 44.6 %collective-permute-start.10 = (f32[1,16,7168]{2,1,0:T(8,128)}, f32[1,16,7168]{2,1,0:T(8,128)}, u32[]{:S(2)}, u32[]{:S(2)}) collective-permute-start(f32[1,16,7168]{2,1,0:T(8,128)} %collective-permute-done.8), channel_id=1, source_target_pairs={{0,30},{2,0},{4,2},{6,4},{8,6},{10,8},{12,10},{14,12},{16,14},{18,... | collective-permute-start | bytes 1376264 | tf_op jit(solution)/shard_map/ppermute | solution.py:29
  274.9 41.4 %collective-permute-start.13 = (f32[1,16,7168]{2,1,0:T(8,128)}, f32[1,16,7168]{2,1,0:T(8,128)}, u32[]{:S(2)}, u32[]{:S(2)}) collective-permute-start(f32[1,16,7168]{2,1,0:T(8,128)} %collective-permute-done.11), channel_id=1, source_target_pairs={{0,2},{2,4},{4,6},{6,8},{8,10},{10,12},{12,14},{14,16},{16,18},{18... | collective-permute-start | bytes 1376264 | tf_op jit(solution)/shard_map/ppermute | solution.py:27
  316.3 16.8 %collective-permute-start.12 = (f32[1,16,7168]{2,1,0:T(8,128)}, f32[1,16,7168]{2,1,0:T(8,128)}, u32[]{:S(2)}, u32[]{:S(2)}) collective-permute-start(f32[1,16,7168]{2,1,0:T(8,128)} %collective-permute-done.10), channel_id=1, source_target_pairs={{0,30},{2,0},{4,2},{6,4},{8,6},{10,8},{12,10},{14,12},{16,14},{18,... | collective-permute-start | bytes 1376264 | tf_op jit(solution)/shard_map/ppermute | solution.py:29
  316.4 16.8 %collective-permute-start.14 = (f32[1,16,7168]{2,1,0:T(8,128)}, f32[1,16,7168]{2,1,0:T(8,128)}, u32[]{:S(2)}, u32[]{:S(2)}) collective-permute-start(f32[1,16,7168]{2,1,0:T(8,128)} %collective-permute-done.13), channel_id=1, source_target_pairs={{0,2},{2,4},{4,6},{6,8},{8,10},{10,12},{12,14},{14,16},{16,18},{18... | collective-permute-start | bytes 1376264 | tf_op jit(solution)/shard_map/ppermute | solution.py:27
  317.9 14.4 %all-to-all-start.1 = ((bf16[2,64,2048]{2,1,0:T(8,128)(2,1)}), bf16[2,64,2048]{2,1,0:T(8,128)(2,1)S(1)}, u32[]{:S(2)}, u32[]{:S(2)}) async-start(bf16[2,64,2048]{2,1,0:T(8,128)(2,1)} %bitcast.10), calls=%async_computation.1 | async-start | bytes 1048576 | tf_op jit(solution)/shard_map/all_to_all | solution.py:90
  (1 other events, 0.8 us)
Sparse Core Ops, SparseCore 0:
  10.1 53.0 all-gather.4
  65.6 111.8 all-gather.6
  243.7 54.2 all-gather.8
